TPU v7x, 32 devices: a whole 2x2x4 slice. The times are simulated.
32 devices in a mesh: dom: 8 (over z, x), cls: 4 (over y, core).
Axes of the slice: x: 2, y: 2, z: 4, core: 2. Of those that a mesh axis runs over, the one named last changes fastest.
Arguments:
- spectra: bfloat16 [512, 128, 512], P(('dom', 'cls')), may hold values from -6 to 6
- ctf: bfloat16 [512, 128], P(('dom', 'cls')), may hold values from -1 to 1
- noise_power: float32 [128], replicated, may hold values from 0.5 to 8
- references: bfloat16 [48, 32, 512], P('cls'), may hold values from -3 to 3
- owner: int32 [512, 1], P(('dom', 'cls')), may hold values from 0 to 3; in each aligned block of 16 rows (0 to 15, 16 to 31, ...) at most 8 rows name the same one
- sub_class: int32 [512], P(('dom', 'cls')), may hold values from 0 to 11
- rotation: int32 [512], P(('dom', 'cls')), may hold values from 0 to 511
Outputs:
- new_refs: float32 [48, 128, 512], P('cls', 'dom')
- log_evidence: float32 [512], P(('dom', 'cls'))
Inputs may be any that keep to these rules, and one draw needn't show every extreme that they name: Among the 16 particles of one device, at most 8 have the same owner, a bound that some block reaches of them.
All inputs are finite; a program needn't handle non-finite values.
Results may differ from a plain program's by a relative error of at most 0.00067.
Values may be sent and summed in bfloat16 or wider, within the bound.
No kernel may reach another device: no remote copies, remote signals or barrier semaphores. Data moves between devices by JAX's collectives and lax.ppermute only.
A program may use at most 128 MiB of HBM per device.

v0:
```python
import math
import jax
import jax.numpy as jnp
from jax import lax
from jax.sharding import PartitionSpec as P


def rotation_table(half, turns_all):
    freq = jnp.arange(half, dtype=jnp.int32)
    steps = jnp.arange(turns_all, dtype=jnp.int32)
    turns = freq[:, None] * steps[None, :] % turns_all
    angle = turns.astype(jnp.float32) * (2.0 * math.pi / turns_all)
    return jnp.concatenate([jnp.cos(angle), -jnp.sin(angle)], axis=0).astype(jnp.bfloat16)


def paired_rows(weighted):
    half = weighted.shape[2] // 2
    direct = jnp.concatenate([weighted[..., :half], weighted[..., half:]], axis=1)
    swapped = jnp.concatenate([weighted[..., half:], -weighted[..., :half]], axis=1)
    return jnp.concatenate([direct, swapped], axis=0)


def piece_scores(paired, cw_low, piece, table):
    half = piece.shape[2] // 2
    count = cw_low.shape[0]
    kinds = piece.shape[0]
    stacked = jnp.concatenate([piece[..., :half], piece[..., half:]], axis=1)
    both = jnp.einsum("nqf,kqf->nkf", paired, stacked, preferred_element_type=jnp.float32)
    cross = jnp.concatenate([both[:count], both[count:]], axis=-1).astype(jnp.bfloat16)
    corr = jnp.dot(
        cross.reshape(count * kinds, 2 * half), table, preferred_element_type=jnp.float32
    )
    corr = corr.reshape(count, kinds, table.shape[1])
    ynorm = jnp.sum(jnp.square(piece.astype(jnp.float32)), axis=-1)
    energy = jnp.dot(cw_low, ynorm.T, precision=lax.Precision.HIGHEST)
    return corr - 0.5 * energy[:, :, None]


def fold_evidence(carry, score):
    top, total = carry
    new_top = jnp.max(score, axis=(1, 2))
    total = total * jnp.exp(top - new_top) + jnp.sum(
        jnp.exp(score - new_top[:, None, None]), axis=(1, 2)
    )
    return (new_top, total)


def align_slots(images, ctf_recv, turn_index, noise, half, turns_all):
    cfl = ctf_recv.astype(jnp.float32)
    wr = cfl / noise
    turns = jnp.arange(half, dtype=jnp.int32) * turn_index[..., None] % turns_all
    angle = turns.astype(jnp.float32) * (2.0 * math.pi / turns_all)
    cosv = jnp.cos(angle)[..., None, :]
    sinv = jnp.sin(angle)[..., None, :]
    values = images.astype(jnp.float32)
    x_re = values[..., :half]
    x_im = values[..., half:]
    a_re = wr[..., None] * (x_re * cosv - x_im * sinv)
    a_im = wr[..., None] * (x_re * sinv + x_im * cosv)
    return (jnp.concatenate([a_re, a_im], axis=-1), cfl * wr)


def per_device(spectra, ctf, noise_power, references, owner, sub_class, rotation):
    count = spectra.shape[0]
    cycles = spectra.shape[1]
    half = spectra.shape[2] // 2
    low_cycles = references.shape[1]
    k_local = references.shape[0]
    turns_all = 2 * half
    shards = lax.axis_size("cls")
    table = rotation_table(half, turns_all)
    weight = ctf.astype(jnp.float32) / noise_power[None, :]
    weighted = (
        weight[:, :low_cycles, None] * spectra[:, :low_cycles, :].astype(jnp.float32)
    ).astype(jnp.bfloat16)
    empty = (jnp.full((count,), -jnp.inf, jnp.float32), jnp.zeros((count,), jnp.float32))
    paired = paired_rows(weighted)
    cw_low = ctf[:, :low_cycles].astype(jnp.float32) * weight[:, :low_cycles]
    top, total = fold_evidence(
        empty,
        piece_scores(paired, cw_low, lax.all_gather(references, "cls", axis=0, tiled=True), table),
    )
    log_evidence = top + jnp.log(total)
    capacity = max(2, 2 * count // shards)
    slots = shards * capacity
    dest = owner[:, 0]
    hit = (dest[:, None] == jnp.arange(shards, dtype=jnp.int32)[None, :]).astype(jnp.int32)
    rank = jnp.sum((jnp.cumsum(hit, axis=0) - hit) * hit, axis=1)
    target = dest * capacity + rank
    place = jnp.arange(slots, dtype=jnp.int32)[:, None] == target[None, :]
    place_half = place.astype(jnp.bfloat16)
    send_img = jnp.dot(
        place_half, spectra.reshape(count, cycles * 2 * half), preferred_element_type=jnp.float32
    )
    send_img = send_img.astype(jnp.bfloat16).reshape(shards, capacity, cycles, 2 * half)
    send_ctf = (
        jnp.dot(place_half, ctf, preferred_element_type=jnp.float32)
        .astype(jnp.bfloat16)
        .reshape(shards, capacity, cycles)
    )
    placed = place.astype(jnp.int32)
    send_meta = jnp.stack(
        [jnp.sum(placed * rotation[None, :], axis=1), jnp.sum(placed * sub_class[None, :], axis=1)],
        axis=-1,
    )
    send_meta = send_meta.reshape(shards, capacity, 2)
    images = lax.all_to_all(send_img, "cls", split_axis=0, concat_axis=0, tiled=True)
    ctf_recv = lax.all_to_all(send_ctf, "cls", split_axis=0, concat_axis=0, tiled=True)
    meta = lax.all_to_all(send_meta, "cls", split_axis=0, concat_axis=0, tiled=True)
    aligned_part, cw_part = align_slots(
        images, ctf_recv, meta[:, :, 0], noise_power, half, turns_all
    )
    local = meta[:, :, 1]
    member = (
        local.reshape(slots)[:, None] == jnp.arange(k_local, dtype=jnp.int32)[None, :]
    ).astype(jnp.float32)
    numer = jnp.dot(
        member.T, aligned_part.reshape(slots, cycles * 2 * half), precision=lax.Precision.HIGHEST
    )
    numer = numer.reshape(k_local, cycles, 2 * half)
    denom = jnp.dot(member.T, cw_part.reshape(slots, cycles), precision=lax.Precision.HIGHEST)
    numer_part, denom_part = (
        lax.psum_scatter(numer, "dom", scatter_dimension=1, tiled=True),
        lax.psum_scatter(denom, "dom", scatter_dimension=1, tiled=True),
    )
    new_refs = numer_part / (denom_part + 1.0)[:, :, None]
    return (new_refs, log_evidence)


def solution(mesh):
    return jax.shard_map(
        per_device,
        mesh=mesh,
        in_specs=(
            P(("dom", "cls"), None, None),
            P(("dom", "cls"), None),
            P(),
            P("cls", None, None),
            P(("dom", "cls"), None),
            P(("dom", "cls")),
            P(("dom", "cls")),
        ),
        out_specs=(P("cls", "dom", None), P(("dom", "cls"))),
        check_vma=False,
    )
```

profile of v0, /device:TPU:0, one launch (start us, length us, event | category | flops | bytes accessed | tf_op | source)
XLA Modules:
  0.0 201.9 jit_solution(9103172688339019743)
XLA Ops:
  8.0 0.7 fusion.41
  8.8 0.8 select_reduce_fusion.2
  9.6 0.7 multiply_add_fusion
  10.3 0.8 select_reduce_fusion.1
  11.2 0.6 copy.32
  11.8 4.3 %all-to-all-start = ((s32[4,8,2]{1,2,0:T(2,128)}), s32[4,8,2]{1,2,0:T(2,128)S(1)}, u32[]{:S(2)}, u32[]{:S(2)}) async-start(s32[4,8,2]{1,2,0:T(2,128)} %copy.32), calls=%async_computation | async-start | bytes 8192 | tf_op jit(solution)/shard_map/all_to_all | solution.py:109
  16.1 1.5 fusion.18
  17.6 2.8 %copy.48 = bf16[2,8,128,512]{3,1,2,0:T(8,128)(2,1)S(1)} copy(bf16[2,8,128,512]{3,2,1,0:T(8,128)(2,1)} %bitcast.40) | data formatting | bytes 4194304
  20.4 3.3 %all-to-all-start.1 = ((bf16[4,8,128]{2,1,0:T(8,128)(2,1)}), bf16[4,8,128]{2,1,0:T(8,128)(2,1)S(1)}, u32[]{:S(2)}, u32[]{:S(2)}) async-start(bf16[4,8,128]{2,1,0:T(8,128)(2,1)} %fusion.18), calls=%async_computation.1 | async-start | bytes 16384 | tf_op jit(solution)/shard_map/all_to_all | solution.py:108
  23.7 3.3 %convolution_convert_fusion = bf16[32,65536]{1,0:T(8,128)(2,1)} fusion(bf16[16,65536]{1,0:T(8,128)(2,1)S(1)} %bitcast.39, s32[16]{0:T(128)S(1)} %multiply_add_fusion), kind=kOutput, calls=%fused_computation | convolution fusion | flops 69206528 | bytes 6291520 | tf_op jit(solution)/shard_map/dot_general | solution.py:92
  27.5 5.0 %all-to-all-start.2 = ((bf16[4,8,128,512]{3,1,2,0:T(8,128)(2,1)}), bf16[4,8,128,512]{3,1,2,0:T(8,128)(2,1)}, u32[]{:S(2)}, u32[]{:S(2)}) async-start(bf16[4,8,128,512]{3,1,2,0:T(8,128)(2,1)} %bitcast.38), calls=%async_computation.2 | async-start | bytes 8388608 | tf_op jit(solution)/shard_map/all_to_all | solution.py:107
  32.7 0.9 convolution_bitcast_fusion
  34.5 54.6 %all-to-all-done.2 = bf16[4,8,128,512]{3,1,2,0:T(8,128)(2,1)} async-done(((bf16[4,8,128,512]{3,1,2,0:T(8,128)(2,1)}), bf16[4,8,128,512]{3,1,2,0:T(8,128)(2,1)}, u32[]{:S(2)}, u32[]{:S(2)}) %all-to-all-start.2) | async-done | bytes 4194336 | tf_op jit(solution)/shard_map/all_to_all | solution.py:107
  89.1 3.4 %convert_element_type.56 = f32[4,8,128,512]{3,1,2,0:T(8,128)S(1)} convert(bf16[4,8,128,512]{3,1,2,0:T(8,128)(2,1)} %all-to-all-done.2) | non-fusion elementwise | flops 2097152 | bytes 12582912 | tf_op jit(solution)/shard_map/convert_element_type | solution.py:55
  92.5 1.4 subtract_multiply_fusion
  93.9 5.3 %fusion = f32[12,128,512]{2,0,1:T(8,128)} fusion(s32[32]{0:T(128)S(1)} %eq.51, f32[4,8,128,256]{3,1,2,0:T(8,128)S(1)} %get-tuple-element.13, f32[4,8,128,256]{3,1,2,0:T(8,128)S(1)} %get-tuple-element.12), kind=kOutput, calls=%fused_computation.1 | convolution fusion | flops 304087424 | bytes 11534464 | tf_op jit(solution)/shard_map/dot_general | solution.py:117
  99.3 1.1 slice.51
  100.4 2.0 copy.46
  102.3 2.9 %negate_convert_fusion = (bf16[256,512]{1,0:T(8,128)(2,1)}, bf16[256,512]{1,0:T(8,128)(2,1)}) fusion(), kind=kLoop, calls=%fused_computation.39 | loop fusion | flops 2228224 | bytes 524288 | tf_op jit(solution)/shard_map/convert.1
  105.7 1.9 fusion.51
  107.6 0.8 copy.43
  108.5 2.6 %fusion.52 = (bf16[48,32,256]{2,1,0:T(8,128)(2,1)}, bf16[48,32,256]{2,1,0:T(8,128)(2,1)}) fusion(bf16[48,32,512]{2,1,0:T(8,128)(2,1)} %all-gather.2.cloned.1.call-done), kind=kLoop, calls=%fused_computation.84 | loop fusion | bytes 3145728 | tf_op jit(solution)/shard_map/slice | solution.py:27
  111.1 3.8 %copy.45 = bf16[48,32,256]{1,0,2:T(8,128)(2,1)S(1)} copy(bf16[48,32,256]{2,1,0:T(8,128)(2,1)} %get-tuple-element.20) | data formatting | bytes 1572864
  114.9 4.9 %copy.44 = bf16[48,32,256]{1,0,2:T(8,128)(2,1)} copy(bf16[48,32,256]{2,1,0:T(8,128)(2,1)} %get-tuple-element.19) | data formatting | bytes 1572864
  119.9 6.0 %convert_bitcast_fusion = bf16[32,48,256]{1,0,2:T(8,128)(2,1)S(1)} fusion(bf16[16,32,256]{1,0,2:T(8,128)(2,1)} %get-tuple-element.17, bf16[16,32,256]{1,0,2:T(8,128)(2,1)} %get-tuple-element.18, bf16[16,32,256]{1,0,2:T(8,128)(2,1)} %get-tuple-element.16, bf16[48,32,256]{1,0,2:T(8,128)(2,1)S(1)} %copy.45, bf16[48,32,256]{1,0,2:T(8,128)(2,1)} %copy.44), kind=kOutput, calls=%fused_computation.20 | convolution fusion | flops 58064896 | bytes 3145728 | tf_op jit(solution)/shard_map/nqf,kqf->nkf/dot_general | solution.py:28
  125.9 1.3 fusion.50
  127.3 2.0 copy.40
  129.3 0.8 copy.39
  130.6 1.7 fusion.53
  133.3 59.0 %reduce-scatter.5.cloned.1.call-done = f32[12,16,512]{2,0,1:T(8,128)} async-done(((f32[12,128,512]{2,0,1:T(8,128)}), f32[12,16,512]{2,0,1:T(8,128)}) %reduce-scatter.5.cloned.1.call-update) | async-done | bytes 393232 | tf_op jit(solution)/shard_map/reduce_scatter | solution.py:123
  192.3 1.1 broadcast_divide_fusion
  193.5 1.0 copy.41
  (33 shorter events, 3.8 us)
Async XLA Ops:
  11.8 8.6 %all-to-all-start = ((s32[4,8,2]{1,2,0:T(2,128)}), s32[4,8,2]{1,2,0:T(2,128)S(1)}, u32[]{:S(2)}, u32[]{:S(2)}) async-start(s32[4,8,2]{1,2,0:T(2,128)} %copy.32), calls=%async_computation | async-start | bytes 8192 | tf_op jit(solution)/shard_map/all_to_all | solution.py:109
  20.4 7.1 %all-to-all-start.1 = ((bf16[4,8,128]{2,1,0:T(8,128)(2,1)}), bf16[4,8,128]{2,1,0:T(8,128)(2,1)S(1)}, u32[]{:S(2)}, u32[]{:S(2)}) async-start(bf16[4,8,128]{2,1,0:T(8,128)(2,1)} %fusion.18), calls=%async_computation.1 | async-start | bytes 16384 | tf_op jit(solution)/shard_map/all_to_all | solution.py:108
  27.5 5.2 %copy-start.2 = (f32[128]{0:T(128)S(1)}, f32[128]{0:T(128)}, u32[]{:S(2)}) copy-start(f32[128]{0:T(128)} %param.9) | copy-start | bytes 1540
  27.5 61.6 %all-to-all-start.2 = ((bf16[4,8,128,512]{3,1,2,0:T(8,128)(2,1)}), bf16[4,8,128,512]{3,1,2,0:T(8,128)(2,1)}, u32[]{:S(2)}, u32[]{:S(2)}) async-start(bf16[4,8,128,512]{3,1,2,0:T(8,128)(2,1)} %bitcast.38), calls=%async_computation.2 | async-start | bytes 8388608 | tf_op jit(solution)/shard_map/all_to_all | solution.py:107
  32.5 75.1 %reduce-scatter.7.cloned.1.call-start = ((), (), s32[]{:S(2)}) async-start(), calls=%async_computation.7 | async-start | bytes 73728
  33.6 74.9 %all-gather.2.cloned.1.call-start = ((), (), s32[]{:S(2)}) async-start(), calls=%async_computation.6 | async-start | bytes 1966080 | tf_op jit(solution)/shard_map/all_gather | solution.py:81
  34.1 158.2 %reduce-scatter.5.cloned.1.call-start = ((), (), s32[]{:S(2)}) async-start(), calls=%async_computation.5 | async-start | bytes 4718592 | tf_op jit(solution)/shard_map/reduce_scatter | solution.py:123
  99.2 6.0 %copy-start.1 = (bf16[16,128]{1,0:T(8,128)(2,1)S(1)}, bf16[16,128]{1,0:T(8,128)(2,1)}, u32[]{:S(2)}) copy-start(bf16[16,128]{1,0:T(8,128)(2,1)} %param.8) | copy-start | bytes 12292
  125.9 4.2 %copy-start = (bf16[48,32,512]{2,1,0:T(8,128)(2,1)S(1)}, bf16[48,32,512]{2,1,0:T(8,128)(2,1)}, u32[]{:S(2)}) copy-start(bf16[48,32,512]{2,1,0:T(8,128)(2,1)} %all-gather.2.cloned.1.call-done) | copy-start | bytes 4718596
Sparse Core Ops, SparseCore 0:
  36.7 64.5 reduce-scatter.6
  104.9 87.3 reduce-scatter.4
Sparse Core Ops, SparseCore 1:
  35.6 30.1 all-gather.1
where the time goes:
time: 203 us; the launch traced here: 202 us
  waiting for transfers between devices  115 us (57%)
  local copies, waits for them, and re-layouts  24.3 us (12%)
  matrix products  19 us (9%)
  other arithmetic  15.7 us (8%)
  between operations  15.6 us (8%)
  starting transfers between devices  12.7 us (6%)
    reduce_scatter x1, waiting for transfers between devices, per_device(): lax.psum_scatter(numer, 'dom', scatter_dimension=1, tiled=True)  59 us
    all_to_all x1, waiting for transfers between devices, per_device(): lax.all_to_all(send_img, 'cls', split_axis=0, concat_axis=0, tiled=True)  54.6 us
    unnamed x12, local copies, waits for them, and re-layouts  15.3 us
    dot_general x1, matrix products, piece_scores(): jnp.einsum('nqf,kqf->nkf', paired, stacked, preferred_element_type=jnp.fl...  6.05 us
    dot_general x1, matrix products, per_device(): jnp.dot(member.T, aligned_part.reshape(slots, cycles * 2 * half), precisi...  5.33 us
    all_to_all x1, starting transfers between devices, per_device(): lax.all_to_all(send_img, 'cls', split_axis=0, concat_axis=0, tiled=True)  4.99 us
    all_to_all x1, starting transfers between devices, per_device(): lax.all_to_all(send_meta, 'cls', split_axis=0, concat_axis=0, tiled=True)  4.26 us
  transfers between devices with their start and end apart: 6, of which 3 were waited for; matrix products, arithmetic and copies ran while one was open for 26% of the time, Pallas kernels for 0%

commit v1 on v0

--- a/solution.py
+++ b/solution.py
@@ -61,6 +61,26 @@
 
 
 def per_device(spectra, ctf, noise_power, references, owner, sub_class, rotation):
+
+    def turn_columns(unit, chip_axis):
+        piece_out, f_next = (lax.axis_size(chip_axis), lax.axis_index(chip_axis))
+        inter = unit.shape[0] // piece_out
+        arr_next = list(unit.shape)
+        arr_next[0] = inter
+        z2 = arr_next[0]
+        arr_next[0] = z2 * piece_out
+        met_up = jnp.zeros(arr_next, unit.dtype)
+        for ii in range(piece_out):
+            base_arr = lax.dynamic_slice_in_dim(unit, (f_next ^ ii) * inter, inter, axis=0)
+            if ii:
+                base_arr = lax.ppermute(
+                    base_arr,
+                    axis_name=chip_axis,
+                    perm=list(map(lambda b: (b, b ^ ii), range(piece_out))),
+                )
+            met_up = lax.dynamic_update_slice_in_dim(met_up, base_arr, (f_next ^ ii) * z2, axis=0)
+        return met_up
+
     count = spectra.shape[0]
     cycles = spectra.shape[1]
     half = spectra.shape[2] // 2
@@ -104,7 +124,7 @@
         axis=-1,
     )
     send_meta = send_meta.reshape(shards, capacity, 2)
-    images = lax.all_to_all(send_img, "cls", split_axis=0, concat_axis=0, tiled=True)
+    images = turn_columns(send_img, "cls")
     ctf_recv = lax.all_to_all(send_ctf, "cls", split_axis=0, concat_axis=0, tiled=True)
     meta = lax.all_to_all(send_meta, "cls", split_axis=0, concat_axis=0, tiled=True)
     aligned_part, cw_part = align_slots(

time: 203 us -> 206 us (1.015)
  local copies, waits for them, and re-layouts: 24.3 us -> 35.6 us
  waiting for transfers between devices: 115 us -> 109 us
  starting transfers between devices: 12.7 us -> 9.5 us
    all_to_all x1 -> x0, waiting for transfers between devices: 54.6 us -> none  [per_device(): lax.all_to_all(send_img, 'cls', split_axis=0, concat_axis=0, tiled=True)]
    ppermute x0 -> x3, waiting for transfers between devices: none -> 47.7 us  [turn_columns(): lax.ppermute(base_arr, axis_name=chip_axis, perm=list(map(lambda b: (b, b...]
    dynamic_update_slice x0 -> x3, local copies, waits for them, and re-layouts: none -> 6.89 us  [turn_columns(): lax.dynamic_update_slice_in_dim(met_up, base_arr, (f_next ^ ii) * z2, axi...]
    all_to_all x1 -> x0, starting transfers between devices: 4.99 us -> none  [per_device(): lax.all_to_all(send_img, 'cls', split_axis=0, concat_axis=0, tiled=True)]
    reduce_scatter x1, waiting for transfers between devices: 59 us -> 54.5 us  [per_device(): lax.psum_scatter(numer, 'dom', scatter_dimension=1, tiled=True)]
    unnamed x12 -> x16, local copies, waits for them, and re-layouts: 15.3 us -> 19.1 us
    all_to_all x1, waiting for transfers between devices: 0.49 us -> 3.62 us  [per_device(): lax.all_to_all(send_ctf, 'cls', split_axis=0, concat_axis=0, tiled=True)]
    all_to_all x1, waiting for transfers between devices: 0.01 us -> 2.25 us  [per_device(): lax.all_to_all(send_meta, 'cls', split_axis=0, concat_axis=0, tiled=True)]
  transfers between devices with their start and end apart: 6 -> 8, of which waited for: 3 -> 6; matrix products, arithmetic and copies ran while one was open for 26% -> 29% of each run, Pallas kernels for 0% -> 0%
where the time goes in v1:
time: 206 us; the launch traced here: 205 us
  waiting for transfers between devices  109 us (53%)
  local copies, waits for them, and re-layouts  35.6 us (17%)
  matrix products  19.6 us (10%)
  other arithmetic  15.7 us (8%)
  between operations  15.7 us (8%)
  starting transfers between devices  9.5 us (5%)
    reduce_scatter x1, waiting for transfers between devices, per_device(): lax.psum_scatter(numer, 'dom', scatter_dimension=1, tiled=True)  54.5 us
    ppermute x3, waiting for transfers between devices, turn_columns(): lax.ppermute(base_arr, axis_name=chip_axis, perm=list(map(lambda b: (b, b...  47.7 us
    unnamed x16, local copies, waits for them, and re-layouts  19.1 us
    dynamic_update_slice x3, local copies, waits for them, and re-layouts, turn_columns(): lax.dynamic_update_slice_in_dim(met_up, base_arr, (f_next ^ ii) * z2, axi...  6.89 us
    dot_general x1, matrix products, piece_scores(): jnp.einsum('nqf,kqf->nkf', paired, stacked, preferred_element_type=jnp.fl...  6.06 us
    dot_general x1, matrix products, per_device(): jnp.dot(member.T, aligned_part.reshape(slots, cycles * 2 * half), precisi...  5.33 us
    all_to_all x1, starting transfers between devices, per_device(): lax.all_to_all(send_meta, 'cls', split_axis=0, concat_axis=0, tiled=True)  4.26 us
  transfers between devices with their start and end apart: 8, of which 6 were waited for; matrix products, arithmetic and copies ran while one was open for 29% of the time, Pallas kernels for 0%

profile of v1, /device:TPU:0, one launch (start us, length us, event | category | flops | bytes accessed | tf_op | source)
XLA Modules:
  0.0 204.8 jit_solution(10233335847039998075)
XLA Ops:
  11.8 4.3 %all-to-all-start = ((s32[4,8,2]{1,2,0:T(2,128)}), s32[4,8,2]{1,2,0:T(2,128)S(1)}, u32[]{:S(2)}, u32[]{:S(2)}) async-start(s32[4,8,2]{1,2,0:T(2,128)} %copy.32), calls=%async_computation | async-start | bytes 8192 | tf_op jit(solution)/shard_map/all_to_all | solution.py:129
  16.1 1.5 fusion.18
  17.6 2.2 %all-to-all-done = s32[4,8,2]{1,2,0:T(2,128)S(1)} async-done(((s32[4,8,2]{1,2,0:T(2,128)}), s32[4,8,2]{1,2,0:T(2,128)S(1)}, u32[]{:S(2)}, u32[]{:S(2)}) %all-to-all-start) | async-done | bytes 288 | tf_op jit(solution)/shard_map/all_to_all | solution.py:129
  19.9 3.2 %all-to-all-start.1 = ((bf16[4,8,128]{2,1,0:T(8,128)(2,1)}), bf16[4,8,128]{2,1,0:T(8,128)(2,1)S(1)}, u32[]{:S(2)}, u32[]{:S(2)}) async-start(bf16[4,8,128]{2,1,0:T(8,128)(2,1)} %fusion.18), calls=%async_computation.1 | async-start | bytes 16384 | tf_op jit(solution)/shard_map/all_to_all | solution.py:128
  23.3 3.6 %all-to-all-done.1 = bf16[4,8,128]{2,1,0:T(8,128)(2,1)S(1)} async-done(((bf16[4,8,128]{2,1,0:T(8,128)(2,1)}), bf16[4,8,128]{2,1,0:T(8,128)(2,1)S(1)}, u32[]{:S(2)}, u32[]{:S(2)}) %all-to-all-start.1) | async-done | bytes 8224 | tf_op jit(solution)/shard_map/all_to_all | solution.py:128
  26.9 1.5 convolution_bitcast_fusion
  29.1 2.8 %copy.48 = bf16[2,8,128,512]{3,1,2,0:T(8,128)(2,1)S(1)} copy(bf16[2,8,128,512]{3,2,1,0:T(8,128)(2,1)} %bitcast.40) | data formatting | bytes 4194304
  31.9 3.3 %convolution_convert_fusion = bf16[32,65536]{1,0:T(8,128)(2,1)} fusion(bf16[16,65536]{1,0:T(8,128)(2,1)S(1)} %bitcast.39, s32[16]{0:T(128)S(1)} %multiply_add_fusion), kind=kOutput, calls=%fused_computation | convolution fusion | flops 69206528 | bytes 6291520 | tf_op jit(solution)/shard_map/dot_general | solution.py:112
  35.5 1.9 copy-done
  37.7 1.9 copy-done.1
  39.7 1.9 collective-permute-start.2
  42.5 2.3 %constant_dynamic-update-slice_fusion.2 = bf16[4,8,128,512]{3,1,2,0:T(8,128)(2,1)} fusion(bf16[4,8,128,512]{3,1,2,0:T(8,128)(2,1)} %copy-done.1, bf16[1,8,128,512]{3,1,2,0:T(8,128)(2,1)} %collective-permute-done, s32[]{:T(128)S(6)} %select_n.39), kind=kLoop, calls=%fused_computation.82 | loop fusion | bytes 2097156 | tf_op jit(solution)/shard_map/dynamic_update_slice | solution.py:81
  44.8 27.1 %collective-permute-done.1 = bf16[1,8,128,512]{3,1,2,0:T(8,128)(2,1)} collective-permute-done((bf16[1,8,128,512]{3,1,2,0:T(8,128)(2,1)S(1)}, bf16[1,8,128,512]{3,1,2,0:T(8,128)(2,1)}, u32[]{:S(2)}, u32[]{:S(2)}) %collective-permute-start.1) | collective-permute-done | bytes 1048608 | tf_op jit(solution)/shard_map/ppermute | solution.py:76
  71.9 2.3 %constant_dynamic-update-slice_fusion.1 = bf16[4,8,128,512]{3,1,2,0:T(8,128)(2,1)} fusion(bf16[4,8,128,512]{3,1,2,0:T(8,128)(2,1)} %constant_dynamic-update-slice_fusion.2, bf16[1,8,128,512]{3,1,2,0:T(8,128)(2,1)} %collective-permute-done.1, s32[]{:T(128)S(6)} %select_n.40), kind=kLoop, calls=%fused_computation.80 | loop fusion | bytes 2097156 | tf_op jit(solution)/shard_map/dynamic_update_slice | solution.py:81
  74.2 20.0 %collective-permute-done.2 = bf16[1,8,128,512]{3,1,2,0:T(8,128)(2,1)} collective-permute-done((bf16[1,8,128,512]{3,1,2,0:T(8,128)(2,1)S(1)}, bf16[1,8,128,512]{3,1,2,0:T(8,128)(2,1)}, u32[]{:S(2)}, u32[]{:S(2)}) %collective-permute-start.2) | collective-permute-done | bytes 1048608 | tf_op jit(solution)/shard_map/ppermute | solution.py:76
  94.2 2.3 %constant_dynamic-update-slice_fusion = bf16[4,8,128,512]{3,1,2,0:T(8,128)(2,1)} fusion(bf16[4,8,128,512]{3,1,2,0:T(8,128)(2,1)} %constant_dynamic-update-slice_fusion.1, bf16[1,8,128,512]{3,1,2,0:T(8,128)(2,1)} %collective-permute-done.2, s32[]{:T(128)S(6)} %select_n.41), kind=kLoop, calls=%fused_computation.78 | loop fusion | bytes 2097156 | tf_op jit(solution)/shard_map/dynamic_update_slice | solution.py:81
  96.5 3.4 %convert_element_type.56 = f32[4,8,128,512]{3,1,2,0:T(8,128)S(1)} convert(bf16[4,8,128,512]{3,1,2,0:T(8,128)(2,1)} %constant_dynamic-update-slice_fusion) | non-fusion elementwise | flops 2097152 | bytes 12582912 | tf_op jit(solution)/shard_map/convert_element_type | solution.py:55
  99.8 1.4 subtract_multiply_fusion
  101.2 5.3 %fusion = f32[12,128,512]{2,0,1:T(8,128)} fusion(s32[32]{0:T(128)S(1)} %eq.51, f32[4,8,128,256]{3,1,2,0:T(8,128)S(1)} %get-tuple-element.13, f32[4,8,128,256]{3,1,2,0:T(8,128)S(1)} %get-tuple-element.12), kind=kOutput, calls=%fused_computation.1 | convolution fusion | flops 304087424 | bytes 11534464 | tf_op jit(solution)/shard_map/dot_general | solution.py:137
  106.6 1.1 slice.51
  107.7 2.0 copy.46
  109.7 2.9 %negate_convert_fusion = (bf16[256,512]{1,0:T(8,128)(2,1)}, bf16[256,512]{1,0:T(8,128)(2,1)}) fusion(), kind=kLoop, calls=%fused_computation.40 | loop fusion | flops 2228224 | bytes 524288 | tf_op jit(solution)/shard_map/convert.1
  113.0 1.9 fusion.51
  115.8 2.6 %fusion.52 = (bf16[48,32,256]{2,1,0:T(8,128)(2,1)}, bf16[48,32,256]{2,1,0:T(8,128)(2,1)}) fusion(bf16[48,32,512]{2,1,0:T(8,128)(2,1)} %all-gather.2.cloned.1.call-done), kind=kLoop, calls=%fused_computation.91 | loop fusion | bytes 3145728 | tf_op jit(solution)/shard_map/slice | solution.py:27
  118.4 3.8 %copy.45 = bf16[48,32,256]{1,0,2:T(8,128)(2,1)S(1)} copy(bf16[48,32,256]{2,1,0:T(8,128)(2,1)} %get-tuple-element.24) | data formatting | bytes 1572864
  122.3 4.9 %copy.44 = bf16[48,32,256]{1,0,2:T(8,128)(2,1)} copy(bf16[48,32,256]{2,1,0:T(8,128)(2,1)} %get-tuple-element.23) | data formatting | bytes 1572864
  127.2 6.1 %convert_bitcast_fusion = bf16[32,48,256]{1,0,2:T(8,128)(2,1)S(1)} fusion(bf16[16,32,256]{1,0,2:T(8,128)(2,1)} %get-tuple-element.21, bf16[16,32,256]{1,0,2:T(8,128)(2,1)} %get-tuple-element.22, bf16[16,32,256]{1,0,2:T(8,128)(2,1)} %get-tuple-element.20, bf16[48,32,256]{1,0,2:T(8,128)(2,1)S(1)} %copy.45, bf16[48,32,256]{1,0,2:T(8,128)(2,1)} %copy.44), kind=kOutput, calls=%fused_computation.20 | convolution fusion | flops 58064896 | bytes 3145728 | tf_op jit(solution)/shard_map/nqf,kqf->nkf/dot_general | solution.py:28
  133.2 1.3 fusion.50
  134.6 2.0 copy.40
  138.0 1.7 fusion.53
  140.7 54.5 %reduce-scatter.5.cloned.1.call-done = f32[12,16,512]{2,0,1:T(8,128)} async-done(((f32[12,128,512]{2,0,1:T(8,128)}), f32[12,16,512]{2,0,1:T(8,128)}) %reduce-scatter.5.cloned.1.call-update) | async-done | bytes 393232 | tf_op jit(solution)/shard_map/reduce_scatter | solution.py:143
  195.2 1.1 broadcast_divide_fusion
  (46 shorter events, 10.7 us)
Async XLA Ops:
  11.8 8.1 %all-to-all-start = ((s32[4,8,2]{1,2,0:T(2,128)}), s32[4,8,2]{1,2,0:T(2,128)S(1)}, u32[]{:S(2)}, u32[]{:S(2)}) async-start(s32[4,8,2]{1,2,0:T(2,128)} %copy.32), calls=%async_computation | async-start | bytes 8192 | tf_op jit(solution)/shard_map/all_to_all | solution.py:129
  19.9 7.0 %all-to-all-start.1 = ((bf16[4,8,128]{2,1,0:T(8,128)(2,1)}), bf16[4,8,128]{2,1,0:T(8,128)(2,1)S(1)}, u32[]{:S(2)}, u32[]{:S(2)}) async-start(bf16[4,8,128]{2,1,0:T(8,128)(2,1)} %fusion.18), calls=%async_computation.1 | async-start | bytes 16384 | tf_op jit(solution)/shard_map/all_to_all | solution.py:128
  23.1 91.8 %reduce-scatter.7.cloned.1.call-start = ((), (), s32[]{:S(2)}) async-start(), calls=%async_computation.6 | async-start | bytes 73728
  28.5 87.3 %all-gather.2.cloned.1.call-start = ((), (), s32[]{:S(2)}) async-start(), calls=%async_computation.5 | async-start | bytes 1966080 | tf_op jit(solution)/shard_map/all_gather | solution.py:101
  29.0 166.2 %reduce-scatter.5.cloned.1.call-start = ((), (), s32[]{:S(2)}) async-start(), calls=%async_computation.4 | async-start | bytes 4718592 | tf_op jit(solution)/shard_map/reduce_scatter | solution.py:143
  35.1 2.3 %copy-start = (bf16[32,65536]{1,0:T(8,128)(2,1)S(1)}, bf16[32,65536]{1,0:T(8,128)(2,1)}, u32[]{:S(2)}) copy-start(bf16[32,65536]{1,0:T(8,128)(2,1)} %convolution_convert_fusion) | copy-start | bytes 12582916
  37.4 4.3 %copy-start.4 = (f32[128]{0:T(128)S(1)}, f32[128]{0:T(128)}, u32[]{:S(2)}) copy-start(f32[128]{0:T(128)} %param.9) | copy-start | bytes 1540
  37.7 1.9 copy-start.1
  39.7 2.8 %collective-permute-start = (bf16[1,8,128,512]{3,1,2,0:T(8,128)(2,1)S(1)}, bf16[1,8,128,512]{3,1,2,0:T(8,128)(2,1)}, u32[]{:S(2)}, u32[]{:S(2)}) collective-permute-start(bf16[1,8,128,512]{3,1,2,0:T(8,128)(2,1)S(1)} %get-tuple-element.16), channel_id=1, source_target_pairs={{0,1},{1,0},{2,3},{3,2},{4,5},{5,4},{6,7},{7,6},{8,9},{9,8},{10,11... | collective-permute-start | bytes 3145736 | tf_op jit(solution)/shard_map/ppermute | solution.py:76
  39.7 32.3 %collective-permute-start.1 = (bf16[1,8,128,512]{3,1,2,0:T(8,128)(2,1)S(1)}, bf16[1,8,128,512]{3,1,2,0:T(8,128)(2,1)}, u32[]{:S(2)}, u32[]{:S(2)}) collective-permute-start(bf16[1,8,128,512]{3,1,2,0:T(8,128)(2,1)S(1)} %get-tuple-element.15), channel_id=1, source_target_pairs={{0,2},{1,3},{2,0},{3,1},{4,6},{5,7},{6,4},{7,5},{8,10},{9,11},{10,... | collective-permute-start | bytes 3145736 | tf_op jit(solution)/shard_map/ppermute | solution.py:76
  39.7 54.5 %collective-permute-start.2 = (bf16[1,8,128,512]{3,1,2,0:T(8,128)(2,1)S(1)}, bf16[1,8,128,512]{3,1,2,0:T(8,128)(2,1)}, u32[]{:S(2)}, u32[]{:S(2)}) collective-permute-start(bf16[1,8,128,512]{3,1,2,0:T(8,128)(2,1)S(1)} %get-tuple-element.14), channel_id=1, source_target_pairs={{0,3},{1,2},{2,1},{3,0},{4,7},{5,6},{6,5},{7,4},{8,11},{9,10},{10,... | collective-permute-start | bytes 3145736 | tf_op jit(solution)/shard_map/ppermute | solution.py:76
  106.6 6.0 %copy-start.3 = (bf16[16,128]{1,0:T(8,128)(2,1)S(1)}, bf16[16,128]{1,0:T(8,128)(2,1)}, u32[]{:S(2)}) copy-start(bf16[16,128]{1,0:T(8,128)(2,1)} %param.8) | copy-start | bytes 12292
  133.2 4.2 %copy-start.2 = (bf16[48,32,512]{2,1,0:T(8,128)(2,1)S(1)}, bf16[48,32,512]{2,1,0:T(8,128)(2,1)}, u32[]{:S(2)}) copy-start(bf16[48,32,512]{2,1,0:T(8,128)(2,1)} %all-gather.2.cloned.1.call-done) | copy-start | bytes 4718596
Sparse Core Ops, SparseCore 0:
  28.6 63.2 reduce-scatter.6
  106.7 88.4 reduce-scatter.4
Sparse Core Ops, SparseCore 1:
  30.5 26.8 all-gather.1
